TPU v7x, 128 devices: a whole 4x4x4 slice. The times are simulated.
128 devices in a mesh: lat: 8 (over y, z_lo), lon: 16 (over z_hi, x, core).
Axes of the slice: x: 4, y: 4, z: 4 (z_hi: 2, z_lo: 2; z = z_hi * 2 + z_lo), core: 2. Of those that a mesh axis runs over, the one named last changes fastest.
Arguments:
- state: bfloat16 [1024, 2048, 128], P('lat', 'lon'), may hold values from -6 to 6
- edge_metric: float32 [9, 1024, 2048], P(None, 'lat', 'lon'), may hold values from 0.1 to 1
- stencil_coef: float32 [2, 9, 128], replicated, may hold values from -4 to 4
- norm_gain: float32 [2, 128], replicated, may hold values from 0.25 to 1.75
- biases: float32 [2, 4, 128], replicated, may hold values from -3 to 3
- weights: bfloat16 [2, 896, 128], P(None, ('lat', 'lon')), may hold values from -0.5 to 0.5
Outputs:
- refined: bfloat16 [1024, 2048, 128], P('lat', 'lon')
All inputs are finite; a program needn't handle non-finite values.
Results may differ from a plain program's by a relative error of at most 0.0069.
Values may be sent and summed in bfloat16 or wider, within the bound.
A program may use at most 128 MiB of HBM per device.

v0:
```python
import jax
import jax.numpy as jnp
from jax import lax
from jax.sharding import PartitionSpec as P

KMAT = 7
ITERS = 2
EPSILON = 1e-05


def extended(cells, sides, width, closed):
    for axis, dim in sides:
        count = lax.axis_size(axis)
        ends = count if closed else count - 1
        head = lax.slice_in_dim(cells, 0, width, axis=dim)
        tail = lax.slice_in_dim(cells, cells.shape[dim] - width, cells.shape[dim], axis=dim)
        cells = jnp.concatenate(
            [
                lax.ppermute(tail, axis, [(i, (i + 1) % count) for i in range(ends)]),
                cells,
                lax.ppermute(head, axis, [((i + 1) % count, i) for i in range(ends)]),
            ],
            axis=dim,
        )
    return cells


def passed_along(block, axis, distance):
    devices = range(lax.axis_size(axis))
    route = [((i - distance) % len(devices), i) for i in devices]
    return lax.ppermute(block, axis, route)


def grid_update(padded_rows, metric_rows, state_rows, coef, gain, bias, mats):
    row_count = state_rows.shape[0]
    col_count = state_rows.shape[1]
    channels = state_rows.shape[2]
    summed = jnp.zeros(state_rows.shape, jnp.float32)
    for lat_step in range(3):
        for lon_step in range(3):
            direction = 3 * lat_step + lon_step
            view = padded_rows[
                lat_step : lat_step + row_count, lon_step : lon_step + col_count
            ].astype(jnp.float32)
            summed = summed + metric_rows[direction][:, :, None] * coef[direction] * view
    scale = lax.rsqrt(jnp.mean(summed * summed, axis=-1, keepdims=True) + EPSILON)
    normed = (summed * scale * gain).astype(jnp.bfloat16).reshape(-1, channels)
    hidden = state_rows.reshape(-1, channels)
    message = (jnp.dot(normed, mats[0], preferred_element_type=jnp.float32) + bias[0]).astype(
        jnp.bfloat16
    )
    update = jax.nn.sigmoid(
        jnp.dot(message, mats[1], preferred_element_type=jnp.float32)
        + jnp.dot(hidden, mats[4], preferred_element_type=jnp.float32)
        + bias[1]
    )
    reset = jax.nn.sigmoid(
        jnp.dot(message, mats[2], preferred_element_type=jnp.float32)
        + jnp.dot(hidden, mats[5], preferred_element_type=jnp.float32)
        + bias[2]
    )
    candidate = jnp.tanh(
        jnp.dot(message, mats[3], preferred_element_type=jnp.float32)
        + bias[3]
        + reset * jnp.dot(hidden, mats[6], preferred_element_type=jnp.float32)
    )
    result = (1.0 - update) * candidate + update * hidden.astype(jnp.float32)
    return result.astype(jnp.bfloat16).reshape(state_rows.shape)


def place_poles(tall, mirrored, band_index, band_count):
    north = jnp.where(band_index == 0, mirrored[0], tall[0])
    south = jnp.where(band_index == band_count - 1, mirrored[1], tall[-1])
    return jnp.concatenate([north[None], tall[1:-1], south[None]], axis=0)


def pad_tile(current, band_index, band_count, half_cycle):
    widened = extended(current, (("lon", 1),), 1, True)
    tall = extended(widened, (("lat", 0),), 1, False)
    mirrored = passed_along(jnp.stack([widened[0], widened[-1]]), "lon", half_cycle)
    return place_poles(tall, mirrored, band_index, band_count)


def on_device(state, edge_metric, stencil_coef, norm_gain, biases, weights):
    gathered = lax.all_gather(weights, ("lat", "lon"), axis=1, tiled=True)
    band_index = lax.axis_index("lat")
    band_count = lax.axis_size("lat")
    half_cycle = lax.axis_size("lon") // 2
    channels = state.shape[2]
    current = state
    for iteration in range(ITERS):
        padded = pad_tile(current, band_index, band_count, half_cycle)
        mats = gathered[iteration].reshape(KMAT, channels, channels)
        current = grid_update(
            padded,
            edge_metric,
            current,
            stencil_coef[iteration],
            norm_gain[iteration],
            biases[iteration],
            mats,
        )
    return current


def solution(mesh):
    in_specs = (
        P("lat", "lon", None),
        P(None, "lat", "lon"),
        P(),
        P(),
        P(),
        P(None, ("lat", "lon"), None),
    )
    out_specs = P("lat", "lon", None)
    return jax.shard_map(
        on_device, mesh=mesh, in_specs=in_specs, out_specs=out_specs, check_vma=False
    )
```

profile of v0, /device:TPU:7, one launch (start us, length us, event | category | flops | bytes accessed | tf_op | source)
XLA Modules:
  0.0 350.3 jit_solution(6598155244749161238)
XLA Ops:
  0.0 1.1 fusion.37
  1.1 4.1 %collective-permute-start = (bf16[128,1,128]{2,1,0:T(2,128)(2,1)S(1)}, bf16[128,1,128]{2,1,0:T(2,128)(2,1)S(1)}, u32[]{:S(2)}, u32[]{:S(2)}) collective-permute-start(bf16[128,1,128]{2,1,0:T(2,128)(2,1)S(1)} %get-tuple-element.19), channel_id=1, source_target_pairs={{0,1},{1,2},{2,3},{3,4},{4,5},{5,6},{6,7},{7,8},{8,9},{9,10},{10,1... | collective-permute-start | bytes 98312 | tf_op jit(solution)/shard_map/ppermute | solution.py:19
  5.3 0.0 collective-permute-start.1
  5.3 1.5 slice_bitcast_fusion.36
  6.8 1.1 slice_bitcast_fusion.8
  7.9 168.0 %all_gather.3 = bf16[2,896,128]{2,0,1:T(2,128)(2,1)S(1)} all-gather(bf16[2,7,128]{2,0,1:T(2,128)(2,1)} %param.11), channel_id=1, replica_groups=mesh['lat'=8,'lon'=16] {'lat','lon'}, dimensions={1}, use_global_device_ids=true | all-gather | bytes 462336 | tf_op jit(solution)/shard_map/all_gather | solution.py:85
  176.0 1.5 fusion.38
  177.4 1.5 slice_bitcast_fusion.11
  178.9 0.0 collective-permute-done
  178.9 0.0 collective-permute-done.1
  178.9 0.8 pad_maximum_fusion.11
  179.7 1.3 collective-permute-start.3
  181.0 0.6 pad_maximum_fusion.6
  181.6 1.3 collective-permute-start.4
  182.9 0.3 collective-permute-start.2
  183.2 0.8 slice_bitcast_fusion.13
  184.0 2.4 collective-permute-done.4
  186.4 2.2 collective-permute-done.2
  188.6 0.8 slice_select_fusion.3
  189.4 9.6 %maximum_maximum_fusion = (bf16[129,130,128]{2,1,0:T(8,128)(2,1)S(1)}, bf16[129,130,128]{2,1,0:T(8,128)(2,1)S(1)}) fusion(bf16[128,1,128]{2,1,0:T(2,128)(2,1)S(1)} %collective-permute-done.1, bf16[128,128,128]{2,1,0:T(8,128)(2,1)} %param.6, bf16[128,1,128]{2,1,0:T(2,128)(2,1)S(1)} %collective-permute-done, bf16[1,130,128]{2,1,0:T(8,128)(2,1)S(1)} %get-tuple-element.46, ...), kind=kLoop, calls=%fused_computation.48 | loop fusion | flops 34344960 | bytes 12912640 | tf_op jit(solution)/shard_map/concatenate | solution.py:74
  199.0 24.2 %multiply_reduce_fusion.1 = (f32[128,128]{1,0:T(8,128)S(1)}, f32[128,128,128]{2,1,0:T(8,128)S(1)}) fusion(bf16[129,130,128]{2,1,0:T(8,128)(2,1)S(1)} %get-tuple-element.14, f32[128]{0:T(128)} %get-tuple-element.55, f32[128,128]{1,0:T(8,128)S(1)} %get-tuple-element.28, f32[128]{0:T(128)} %get-tuple-element.56, f32[128,128]{1,0:T(8,128)S(1)} %get-tuple-element.29, ...), kind=kLoop, calls=%fused_computation.46 | loop fusion | flops 90161152 | bytes 38474240 | tf_op jit(solution)/shard_map/reduce_sum | solution.py:46
  223.3 4.7 %multiply_convert_fusion.1 = bf16[128,128,128]{2,1,0:T(8,128)(2,1)S(1)} fusion(f32[128,128,128]{2,1,0:T(8,128)S(1)} %get-tuple-element.8, f32[128]{0:T(128)S(1)} %get-tuple-element.75, f32[128,128]{1,0:T(8,128)S(1)} %add_rsqrt_fusion.1), kind=kLoop, calls=%fused_computation.45 | loop fusion | flops 6291456 | bytes 12648960 | tf_op jit(solution)/shard_map/convert_element_type | solution.py:47
  228.0 1.2 fusion.26
  229.2 1.2 fusion.35
  230.5 1.2 fusion.34
  231.7 4.5 %convolution_add_fusion.5 = f32[16384,128]{1,0:T(8,128)} fusion(bf16[16384,128]{1,0:T(8,128)(2,1)S(1)} %fusion.26, f32[128]{0:T(128)S(1)} %get-tuple-element.69, bf16[1,128,128]{2,0,1:T(2,128)(2,1)S(1)} %get-tuple-element.40), kind=kOutput, calls=%fused_computation.25 | convolution fusion | flops 538968064 | bytes 12616192 | tf_op jit(solution)/shard_map/dot_general | solution.py:63
  236.3 4.5 %fusion.28 = f32[16384,128]{1,0:T(8,128)} fusion(f32[16384,128]{1,0:T(8,128)S(1)} %fusion.35, bf16[16384,128]{1,0:T(8,128)(2,1)S(1)} %bitcast.139, f32[128]{0:T(128)S(1)} %copy-done.17, bf16[1,128,128]{2,0,1:T(2,128)(2,1)S(1)} %copy-done.4), kind=kOutput, calls=%fused_computation.38 | convolution fusion | flops 547356672 | bytes 21004800 | tf_op jit(solution)/shard_map/dot_general | solution.py:54
  240.8 4.6 %fusion.29 = f32[16384,128]{1,0:T(8,128)} fusion(f32[16384,128]{1,0:T(8,128)S(1)} %fusion.34, bf16[16384,128]{1,0:T(8,128)(2,1)S(1)} %bitcast.140, f32[128]{0:T(128)S(1)} %copy-done.16, bf16[1,128,128]{2,0,1:T(2,128)(2,1)S(1)} %copy-done.3), kind=kOutput, calls=%fused_computation.39 | convolution fusion | flops 547356672 | bytes 21004800 | tf_op jit(solution)/shard_map/dot_general | solution.py:59
  245.4 9.8 %fusion.25 = bf16[16384,128]{1,0:T(8,128)(2,1)S(1)} fusion(f32[16384,128]{1,0:T(8,128)} %convolution_add_fusion.5, f32[16384,128]{1,0:T(8,128)} %fusion.29, bf16[16384,128]{1,0:T(8,128)(2,1)S(1)} %bitcast.141, f32[16384,128]{1,0:T(8,128)} %fusion.28, bf16[1,128,128]{2,0,1:T(2,128)(2,1)S(1)} %get-tuple-element.37), kind=kOutput, calls=%fused_computation.35 | convolution fusion | flops 553648128 | bytes 33587200 | tf_op jit(solution)/shard_map/dot_general | solution.py:65
  255.2 0.1 fusion.36
  255.3 11.3 %collective-permute-start.5 = (bf16[128,1,128]{2,1,0:T(2,128)(2,1)S(1)}, bf16[128,1,128]{2,1,0:T(2,128)(2,1)S(1)}, u32[]{:S(2)}, u32[]{:S(2)}) collective-permute-start(bf16[128,1,128]{2,1,0:T(2,128)(2,1)S(1)} %get-tuple-element.17), channel_id=1, source_target_pairs={{0,1},{1,2},{2,3},{3,4},{4,5},{5,6},{6,7},{7,8},{8,9},{9,10},{10,1... | collective-permute-start | bytes 98312 | tf_op jit(solution)/shard_map/ppermute | solution.py:19
  266.7 0.1 collective-permute-start.6
  266.8 1.2 collective-permute-done.5
  268.0 6.1 %collective-permute-done.6 = bf16[128,1,128]{2,1,0:T(2,128)(2,1)S(1)} collective-permute-done((bf16[128,1,128]{2,1,0:T(2,128)(2,1)S(1)}, bf16[128,1,128]{2,1,0:T(2,128)(2,1)S(1)}, u32[]{:S(2)}, u32[]{:S(2)}) %collective-permute-start.6) | collective-permute-done | bytes 32800 | tf_op jit(solution)/shard_map/ppermute | solution.py:21
  274.1 3.0 collective-permute-start.7
  277.2 4.1 %collective-permute-start.8 = (bf16[1,130,128]{2,1,0:T(8,128)(2,1)S(1)}, bf16[1,130,128]{2,1,0:T(8,128)(2,1)S(1)}, u32[]{:S(2)}, u32[]{:S(2)}) collective-permute-start(bf16[1,130,128]{2,1,0:T(8,128)(2,1)S(1)} %get-tuple-element.11), channel_id=1, source_target_pairs={{0,16},{16,32},{32,48},{48,64},{64,80},{80,96},{96,112},{1,17},{17... | collective-permute-start | bytes 99848 | tf_op jit(solution)/shard_map/ppermute | solution.py:19
  281.3 1.3 collective-permute-start.9
  282.6 3.4 collective-permute-done.9
  286.0 6.8 %maximum_maximum_fusion.1 = (bf16[129,130,128]{2,1,0:T(8,128)(2,1)S(1)}, bf16[129,130,128]{2,1,0:T(8,128)(2,1)S(1)}) fusion(bf16[128,1,128]{2,1,0:T(2,128)(2,1)S(1)} %collective-permute-done.6, bf16[128,128,128]{2,1,0:T(8,128)(2,1)S(1)} %bitcast.137, bf16[128,1,128]{2,1,0:T(2,128)(2,1)S(1)} %collective-permute-done.5, ...), kind=kLoop, calls=%fused_computation.50 | loop fusion | flops 34344960 | bytes 12912640 | tf_op jit(solution)/shard_map/concatenate | solution.py:74
  293.0 23.4 %multiply_reduce_fusion = (f32[128,128]{1,0:T(8,128)S(1)}, f32[128,128,128]{2,1,0:T(8,128)S(1)}) fusion(bf16[129,130,128]{2,1,0:T(8,128)(2,1)S(1)} %get-tuple-element.10, f32[128]{0:T(128)S(1)} %copy-done.12, f32[128,128]{1,0:T(8,128)S(1)} %get-tuple-element.28, f32[128]{0:T(128)S(1)} %copy-done.13, f32[128,128]{1,0:T(8,128)S(1)} %get-tuple-element.29, ...), kind=kLoop, calls=%fused_computation.43 | loop fusion | flops 90161152 | bytes 38474240 | tf_op jit(solution)/shard_map/reduce_sum | solution.py:46
  316.4 4.7 %multiply_convert_fusion = bf16[128,128,128]{2,1,0:T(8,128)(2,1)S(1)} fusion(f32[128,128,128]{2,1,0:T(8,128)S(1)} %get-tuple-element.6, f32[128]{0:T(128)S(1)} %get-tuple-element.74, f32[128,128]{1,0:T(8,128)S(1)} %add_rsqrt_fusion), kind=kLoop, calls=%fused_computation.42 | loop fusion | flops 6291456 | bytes 12648960 | tf_op jit(solution)/shard_map/convert_element_type | solution.py:47
  321.1 1.2 fusion.27
  322.3 1.2 fusion.33
  323.6 1.2 fusion.32
  324.8 4.5 %convolution_add_fusion.1 = f32[16384,128]{1,0:T(8,128)} fusion(bf16[16384,128]{1,0:T(8,128)(2,1)S(1)} %fusion.27, f32[128]{0:T(128)S(1)} %get-tuple-element.73, bf16[1,128,128]{2,0,1:T(2,128)(2,1)S(1)} %get-tuple-element.33), kind=kOutput, calls=%fused_computation.9 | convolution fusion | flops 538968064 | bytes 12616192 | tf_op jit(solution)/shard_map/dot_general | solution.py:63
  329.4 4.5 %fusion.30 = f32[16384,128]{1,0:T(8,128)} fusion(f32[16384,128]{1,0:T(8,128)S(1)} %fusion.33, bf16[16384,128]{1,0:T(8,128)(2,1)S(1)} %fusion.25, f32[128]{0:T(128)S(1)} %copy-done.15, bf16[1,128,128]{2,0,1:T(2,128)(2,1)S(1)} %copy-done.2), kind=kOutput, calls=%fused_computation.40 | convolution fusion | flops 547356672 | bytes 21004800 | tf_op jit(solution)/shard_map/dot_general | solution.py:54
  333.9 4.6 %fusion.31 = f32[16384,128]{1,0:T(8,128)} fusion(f32[16384,128]{1,0:T(8,128)S(1)} %fusion.32, bf16[16384,128]{1,0:T(8,128)(2,1)S(1)} %fusion.25, f32[128]{0:T(128)S(1)} %copy-done.14, bf16[1,128,128]{2,0,1:T(2,128)(2,1)S(1)} %copy-done.1), kind=kOutput, calls=%fused_computation.41 | convolution fusion | flops 547356672 | bytes 21004800 | tf_op jit(solution)/shard_map/dot_general | solution.py:59
  338.5 11.8 %fusion.24 = bf16[16384,128]{1,0:T(8,128)(2,1)} fusion(f32[16384,128]{1,0:T(8,128)} %convolution_add_fusion.1, f32[16384,128]{1,0:T(8,128)} %fusion.31, bf16[16384,128]{1,0:T(8,128)(2,1)S(1)} %fusion.25, f32[16384,128]{1,0:T(8,128)} %fusion.30, bf16[1,128,128]{2,0,1:T(2,128)(2,1)S(1)} %get-tuple-element.30), kind=kOutput, calls=%fused_computation.34 | convolution fusion | flops 553648128 | bytes 33587200 | tf_op jit(solution)/shard_map/dot_general | solution.py:65
  (44 shorter events, 0.2 us)
Async XLA Ops:
  1.1 177.7 %collective-permute-start = (bf16[128,1,128]{2,1,0:T(2,128)(2,1)S(1)}, bf16[128,1,128]{2,1,0:T(2,128)(2,1)S(1)}, u32[]{:S(2)}, u32[]{:S(2)}) collective-permute-start(bf16[128,1,128]{2,1,0:T(2,128)(2,1)S(1)} %get-tuple-element.19), channel_id=1, source_target_pairs={{0,1},{1,2},{2,3},{3,4},{4,5},{5,6},{6,7},{7,8},{8,9},{9,10},{10,1... | collective-permute-start | bytes 98312 | tf_op jit(solution)/shard_map/ppermute | solution.py:19
  5.3 173.6 %collective-permute-start.1 = (bf16[128,1,128]{2,1,0:T(2,128)(2,1)S(1)}, bf16[128,1,128]{2,1,0:T(2,128)(2,1)S(1)}, u32[]{:S(2)}, u32[]{:S(2)}) collective-permute-start(bf16[128,1,128]{2,1,0:T(2,128)(2,1)S(1)} %get-tuple-element.20), channel_id=1, source_target_pairs={{1,0},{2,1},{3,2},{4,3},{5,4},{6,5},{7,6},{8,7},{9,8},{10,9},{11,1... | collective-permute-start | bytes 98312 | tf_op jit(solution)/shard_map/ppermute | solution.py:21
  179.7 4.3 %collective-permute-start.3 = (bf16[1,130,128]{2,1,0:T(8,128)(2,1)S(1)}, bf16[1,130,128]{2,1,0:T(8,128)(2,1)S(1)}, u32[]{:S(2)}, u32[]{:S(2)}) collective-permute-start(bf16[1,130,128]{2,1,0:T(8,128)(2,1)S(1)} %get-tuple-element.15), channel_id=1, source_target_pairs={{0,16},{16,32},{32,48},{48,64},{64,80},{80,96},{96,112},{1,17},{17... | collective-permute-start | bytes 99848 | tf_op jit(solution)/shard_map/ppermute | solution.py:19
  181.6 4.8 %collective-permute-start.4 = (bf16[1,130,128]{2,1,0:T(8,128)(2,1)S(1)}, bf16[1,130,128]{2,1,0:T(8,128)(2,1)}, u32[]{:S(2)}, u32[]{:S(2)}) collective-permute-start(bf16[1,130,128]{2,1,0:T(8,128)(2,1)S(1)} %get-tuple-element.16), channel_id=1, source_target_pairs={{16,0},{32,16},{48,32},{64,48},{80,64},{96,80},{112,96},{17,1},{33... | collective-permute-start | bytes 99848 | tf_op jit(solution)/shard_map/ppermute | solution.py:21
  182.9 5.7 %collective-permute-start.2 = (bf16[2,130,128]{2,1,0:T(8,128)(2,1)}, bf16[2,130,128]{2,1,0:T(8,128)(2,1)}, u32[]{:S(2)}, u32[]{:S(2)}) collective-permute-start(bf16[2,130,128]{2,1,0:T(8,128)(2,1)} %pad_maximum_fusion.6), channel_id=1, source_target_pairs={{8,0},{9,1},{10,2},{11,3},{12,4},{13,5},{14,6},{15,7},{0,8},{1,9},... | collective-permute-start | bytes 199688 | tf_op jit(solution)/shard_map/ppermute | solution.py:31
  184.0 15.0 %copy-start = (bf16[128,128,128]{2,1,0:T(8,128)(2,1)S(1)}, bf16[128,128,128]{2,1,0:T(8,128)(2,1)}, u32[]{:S(2)}) copy-start(bf16[128,128,128]{2,1,0:T(8,128)(2,1)} %param.6) | copy-start | bytes 12582916
  231.7 4.5 %copy-start.4 = (bf16[1,128,128]{2,0,1:T(2,128)(2,1)S(1)}, bf16[1,128,128]{2,0,1:T(2,128)(2,1)}, u32[]{:S(2)}) copy-start(bf16[1,128,128]{2,0,1:T(2,128)(2,1)} %get-tuple-element.41) | copy-start | bytes 98308
  231.7 4.5 %copy-start.17 = (f32[128]{0:T(128)S(1)}, f32[128]{0:T(128)}, u32[]{:S(2)}) copy-start(f32[128]{0:T(128)} %get-tuple-element.70) | copy-start | bytes 1540
  236.3 4.6 %copy-start.3 = (bf16[1,128,128]{2,0,1:T(2,128)(2,1)S(1)}, bf16[1,128,128]{2,0,1:T(2,128)(2,1)}, u32[]{:S(2)}) copy-start(bf16[1,128,128]{2,0,1:T(2,128)(2,1)} %get-tuple-element.38) | copy-start | bytes 98308
  236.3 4.6 %copy-start.16 = (f32[128]{0:T(128)S(1)}, f32[128]{0:T(128)}, u32[]{:S(2)}) copy-start(f32[128]{0:T(128)} %get-tuple-element.68) | copy-start | bytes 1540
  255.3 12.7 %collective-permute-start.5 = (bf16[128,1,128]{2,1,0:T(2,128)(2,1)S(1)}, bf16[128,1,128]{2,1,0:T(2,128)(2,1)S(1)}, u32[]{:S(2)}, u32[]{:S(2)}) collective-permute-start(bf16[128,1,128]{2,1,0:T(2,128)(2,1)S(1)} %get-tuple-element.17), channel_id=1, source_target_pairs={{0,1},{1,2},{2,3},{3,4},{4,5},{5,6},{6,7},{7,8},{8,9},{9,10},{10,1... | collective-permute-start | bytes 98312 | tf_op jit(solution)/shard_map/ppermute | solution.py:19
  266.6 26.2 %copy-start.5 = (f32[128]{0:T(128)S(1)}, f32[128]{0:T(128)}, u32[]{:S(2)}) copy-start(f32[128]{0:T(128)} %get-tuple-element.48) | copy-start | bytes 1540
  266.6 26.3 %copy-start.6 = (f32[128]{0:T(128)S(1)}, f32[128]{0:T(128)}, u32[]{:S(2)}) copy-start(f32[128]{0:T(128)} %get-tuple-element.49) | copy-start | bytes 1540
  266.6 26.3 %copy-start.7 = (f32[128]{0:T(128)S(1)}, f32[128]{0:T(128)}, u32[]{:S(2)}) copy-start(f32[128]{0:T(128)} %get-tuple-element.50) | copy-start | bytes 1540
  266.6 26.3 %copy-start.8 = (f32[128]{0:T(128)S(1)}, f32[128]{0:T(128)}, u32[]{:S(2)}) copy-start(f32[128]{0:T(128)} %get-tuple-element.51) | copy-start | bytes 1540
  266.6 26.3 %copy-start.9 = (f32[128]{0:T(128)S(1)}, f32[128]{0:T(128)}, u32[]{:S(2)}) copy-start(f32[128]{0:T(128)} %get-tuple-element.52) | copy-start | bytes 1540
  266.7 26.3 %copy-start.10 = (f32[128]{0:T(128)S(1)}, f32[128]{0:T(128)}, u32[]{:S(2)}) copy-start(f32[128]{0:T(128)} %get-tuple-element.53) | copy-start | bytes 1540
  266.7 26.3 %copy-start.11 = (f32[128]{0:T(128)S(1)}, f32[128]{0:T(128)}, u32[]{:S(2)}) copy-start(f32[128]{0:T(128)} %get-tuple-element.54) | copy-start | bytes 1540
  266.7 26.3 %copy-start.12 = (f32[128]{0:T(128)S(1)}, f32[128]{0:T(128)}, u32[]{:S(2)}) copy-start(f32[128]{0:T(128)} %get-tuple-element.64) | copy-start | bytes 1540
  266.7 26.3 %copy-start.13 = (f32[128]{0:T(128)S(1)}, f32[128]{0:T(128)}, u32[]{:S(2)}) copy-start(f32[128]{0:T(128)} %get-tuple-element.65) | copy-start | bytes 1540
  266.7 7.4 %collective-permute-start.6 = (bf16[128,1,128]{2,1,0:T(2,128)(2,1)S(1)}, bf16[128,1,128]{2,1,0:T(2,128)(2,1)S(1)}, u32[]{:S(2)}, u32[]{:S(2)}) collective-permute-start(bf16[128,1,128]{2,1,0:T(2,128)(2,1)S(1)} %get-tuple-element.18), channel_id=1, source_target_pairs={{1,0},{2,1},{3,2},{4,3},{5,4},{6,5},{7,6},{8,7},{9,8},{10,9},{11,1... | collective-permute-start | bytes 98312 | tf_op jit(solution)/shard_map/ppermute | solution.py:21
  274.1 11.9 %collective-permute-start.7 = (bf16[2,130,128]{2,1,0:T(8,128)(2,1)S(1)}, bf16[2,130,128]{2,1,0:T(8,128)(2,1)S(1)}, u32[]{:S(2)}, u32[]{:S(2)}) collective-permute-start(bf16[2,130,128]{2,1,0:T(8,128)(2,1)S(1)} %pad_maximum_fusion.7), channel_id=1, source_target_pairs={{8,0},{9,1},{10,2},{11,3},{12,4},{13,5},{14,6},{15,7},{0,8},{1,9},... | collective-permute-start | bytes 199688 | tf_op jit(solution)/shard_map/ppermute | solution.py:31
  277.2 5.5 %collective-permute-start.8 = (bf16[1,130,128]{2,1,0:T(8,128)(2,1)S(1)}, bf16[1,130,128]{2,1,0:T(8,128)(2,1)S(1)}, u32[]{:S(2)}, u32[]{:S(2)}) collective-permute-start(bf16[1,130,128]{2,1,0:T(8,128)(2,1)S(1)} %get-tuple-element.11), channel_id=1, source_target_pairs={{0,16},{16,32},{32,48},{48,64},{64,80},{80,96},{96,112},{1,17},{17... | collective-permute-start | bytes 99848 | tf_op jit(solution)/shard_map/ppermute | solution.py:19
  281.3 4.7 %collective-permute-start.9 = (bf16[1,130,128]{2,1,0:T(8,128)(2,1)S(1)}, bf16[1,130,128]{2,1,0:T(8,128)(2,1)S(1)}, u32[]{:S(2)}, u32[]{:S(2)}) collective-permute-start(bf16[1,130,128]{2,1,0:T(8,128)(2,1)S(1)} %get-tuple-element.12), channel_id=1, source_target_pairs={{16,0},{32,16},{48,32},{64,48},{80,64},{96,80},{112,96},{17,1},{33... | collective-permute-start | bytes 99848 | tf_op jit(solution)/shard_map/ppermute | solution.py:21
  324.8 4.5 %copy-start.2 = (bf16[1,128,128]{2,0,1:T(2,128)(2,1)S(1)}, bf16[1,128,128]{2,0,1:T(2,128)(2,1)}, u32[]{:S(2)}) copy-start(bf16[1,128,128]{2,0,1:T(2,128)(2,1)} %get-tuple-element.34) | copy-start | bytes 98308
  324.8 4.5 %copy-start.15 = (f32[128]{0:T(128)S(1)}, f32[128]{0:T(128)}, u32[]{:S(2)}) copy-start(f32[128]{0:T(128)} %get-tuple-element.66) | copy-start | bytes 1540
  329.4 4.6 %copy-start.1 = (bf16[1,128,128]{2,0,1:T(2,128)(2,1)S(1)}, bf16[1,128,128]{2,0,1:T(2,128)(2,1)}, u32[]{:S(2)}) copy-start(bf16[1,128,128]{2,0,1:T(2,128)(2,1)} %get-tuple-element.31) | copy-start | bytes 98308
  329.4 4.6 %copy-start.14 = (f32[128]{0:T(128)S(1)}, f32[128]{0:T(128)}, u32[]{:S(2)}) copy-start(f32[128]{0:T(128)} %get-tuple-element.72) | copy-start | bytes 1540
where the time goes:
time: 351 us; the launch traced here: 350 us
  blocking collectives  168 us (48%)
  other arithmetic  75.8 us (22%)
  matrix products  56.3 us (16%)
  starting transfers between devices  26.9 us (8%)
  waiting for transfers between devices  15.3 us (4%)
  local copies, waits for them, and re-layouts  7.64 us (2%)
    all_gather x1, blocking collectives, on_device(): gathered = lax.all_gather(weights, ('lat', 'lon'), axis=1, tiled=True)  168 us
    reduce_sum x2, other arithmetic, grid_update(): jnp.mean(summed * summed, axis=-1, keepdims=True) + EPSILON  47.6 us
    dot_general x2, matrix products, grid_update(): jnp.dot(hidden, mats[6], preferred_element_type=jnp.float32)  21.6 us
    ppermute x4, starting transfers between devices, extended(): lax.ppermute(tail, axis, [(i, (i + 1) % count) for i in range(ends)])  20.9 us
    concatenate x2, other arithmetic, place_poles(): return jnp.concatenate([north[None], tall[1:-1], south[None]], axis=0)  16.4 us
    ppermute x4, waiting for transfers between devices, extended(): lax.ppermute(head, axis, [((i + 1) % count, i) for i in range(ends)])  11.9 us
    convert_element_type x2, other arithmetic, grid_update(): normed = (summed * scale * gain).astype(jnp.bfloat16).reshape(-1, channels)  9.45 us
    dot_general x2, matrix products, grid_update(): jnp.dot(hidden, mats[5], preferred_element_type=jnp.float32)  9.18 us
  transfers between devices with their start and end apart: 10, of which 5 were waited for; matrix products, arithmetic and copies ran while one was open for 2% of the time, Pallas kernels for 0%

commit v1 on v0

--- a/solution.py
+++ b/solution.py
@@ -82,7 +82,10 @@
 
 
 def on_device(state, edge_metric, stencil_coef, norm_gain, biases, weights):
-    gathered = lax.all_gather(weights, ("lat", "lon"), axis=1, tiled=True)
+    n_dev = lax.axis_size(("lat", "lon"))
+    pieces = jnp.stack([weights for _ in range(n_dev)])
+    pieces = lax.all_to_all(pieces, ("lat", "lon"), split_axis=0, concat_axis=0)
+    gathered = jnp.concatenate(pieces, axis=1)
     band_index = lax.axis_index("lat")
     band_count = lax.axis_size("lat")
     half_cycle = lax.axis_size("lon") // 2

time: 351 us -> 190 us (0.54)
  blocking collectives: 168 us -> 0 us
  starting transfers between devices: 26.9 us -> 31.8 us
    all_gather x1 -> x0, blocking collectives: 168 us -> none  [on_device(): gathered = lax.all_gather(weights, ('lat', 'lon'), axis=1, tiled=True)]
    all_to_all x0 -> x1, starting transfers between devices: none -> 9.58 us  [on_device(): pieces = lax.all_to_all(pieces, ('lat', 'lon'), split_axis=0, concat_axis=0)]
    ppermute x4, starting transfers between devices: 20.9 us -> 16.5 us  [extended(): lax.ppermute(tail, axis, [(i, (i + 1) % count) for i in range(ends)])]
  transfers between devices with their start and end apart: 10 -> 11, of which waited for: 5 -> 4; matrix products, arithmetic and copies ran while one was open for 2% -> 23% of each run, Pallas kernels for 0% -> 0%
where the time goes in v1:
time: 190 us; the launch traced here: 188 us
  other arithmetic  76 us (40%)
  matrix products  58.3 us (31%)
  starting transfers between devices  31.8 us (17%)
  waiting for transfers between devices  12.3 us (6%)
  local copies, waits for them, and re-layouts  9.2 us (5%)
    reduce_sum x2, other arithmetic, grid_update(): jnp.mean(summed * summed, axis=-1, keepdims=True) + EPSILON  46.7 us
    dot_general x2, matrix products, grid_update(): jnp.dot(hidden, mats[6], preferred_element_type=jnp.float32)  21.6 us
    concatenate x2, other arithmetic, place_poles(): return jnp.concatenate([north[None], tall[1:-1], south[None]], axis=0)  19.2 us
    ppermute x4, starting transfers between devices, extended(): lax.ppermute(tail, axis, [(i, (i + 1) % count) for i in range(ends)])  16.5 us
    ppermute x4, waiting for transfers between devices, extended(): lax.ppermute(head, axis, [((i + 1) % count, i) for i in range(ends)])  9.95 us
    all_to_all x1, starting transfers between devices, on_device(): pieces = lax.all_to_all(pieces, ('lat', 'lon'), split_axis=0, concat_axis=0)  9.58 us
    dot_general x2, matrix products, grid_update(): jnp.dot(hidden, mats[4], preferred_element_type=jnp.float32)  9.09 us
    convert_element_type x2, other arithmetic, grid_update(): normed = (summed * scale * gain).astype(jnp.bfloat16).reshape(-1, channels)  9.06 us
  transfers between devices with their start and end apart: 11, of which 4 were waited for; matrix products, arithmetic and copies ran while one was open for 23% of the time, Pallas kernels for 0%

profile of v1, /device:TPU:7, one launch (start us, length us, event | category | flops | bytes accessed | tf_op | source)
XLA Modules:
  0.0 187.8 jit_solution(7713991925421806236)
XLA Ops:
  0.0 1.1 fusion.37
  1.1 4.1 %collective-permute-start = (bf16[128,1,128]{2,1,0:T(2,128)(2,1)S(1)}, bf16[128,1,128]{2,1,0:T(2,128)(2,1)S(1)}, u32[]{:S(2)}, u32[]{:S(2)}) collective-permute-start(bf16[128,1,128]{2,1,0:T(2,128)(2,1)S(1)} %get-tuple-element.21), channel_id=1, source_target_pairs={{0,1},{1,2},{2,3},{3,4},{4,5},{5,6},{6,7},{7,8},{8,9},{9,10},{10,1... | collective-permute-start | bytes 98312 | tf_op jit(solution)/shard_map/ppermute | solution.py:19
  5.3 0.0 collective-permute-start.1
  5.3 1.7 stack.7
  7.0 9.6 %all-to-all-start = ((bf16[128,2,7,128]{3,1,2,0:T(2,128)(2,1)}), bf16[128,2,7,128]{3,1,2,0:T(2,128)(2,1)S(1)}, u32[]{:S(2)}, u32[]{:S(2)}) async-start(bf16[128,2,7,128]{3,1,2,0:T(2,128)(2,1)} %stack.7), calls=%async_computation | async-start | bytes 917504 | tf_op jit(solution)/shard_map/all_to_all | solution.py:87
  16.6 0.9 slice_bitcast_fusion.64
  17.4 1.1 slice_bitcast_fusion.8
  18.6 0.9 slice_bitcast_fusion.39
  19.5 0.8 pad_maximum_fusion.11
  20.3 3.3 %collective-permute-start.3 = (bf16[1,130,128]{2,1,0:T(8,128)(2,1)S(1)}, bf16[1,130,128]{2,1,0:T(8,128)(2,1)S(1)}, u32[]{:S(2)}, u32[]{:S(2)}) collective-permute-start(bf16[1,130,128]{2,1,0:T(8,128)(2,1)S(1)} %get-tuple-element.17), channel_id=1, source_target_pairs={{0,16},{16,32},{32,48},{48,64},{64,80},{80,96},{96,112},{1,17},{17... | collective-permute-start | bytes 99848 | tf_op jit(solution)/shard_map/ppermute | solution.py:19
  23.6 1.3 collective-permute-start.4
  24.9 3.0 %collective-permute-start.2 = (bf16[2,130,128]{2,1,0:T(8,128)(2,1)S(1)}, bf16[2,130,128]{2,1,0:T(8,128)(2,1)S(1)}, u32[]{:S(2)}, u32[]{:S(2)}) collective-permute-start(bf16[2,130,128]{2,1,0:T(8,128)(2,1)S(1)} %pad_maximum_fusion.6), channel_id=1, source_target_pairs={{8,0},{9,1},{10,2},{11,3},{12,4},{13,5},{14,6},{15,7},{0,8},{1,9},... | collective-permute-start | bytes 199688 | tf_op jit(solution)/shard_map/ppermute | solution.py:31
  27.9 0.8 slice_bitcast_fusion.41
  28.7 1.0 collective-permute-done.2
  29.6 9.6 %maximum_maximum_fusion = (bf16[129,130,128]{2,1,0:T(8,128)(2,1)S(1)}, bf16[129,130,128]{2,1,0:T(8,128)(2,1)S(1)}) fusion(bf16[128,1,128]{2,1,0:T(2,128)(2,1)S(1)} %collective-permute-done.1, bf16[128,128,128]{2,1,0:T(8,128)(2,1)} %param.6, bf16[128,1,128]{2,1,0:T(2,128)(2,1)S(1)} %collective-permute-done, bf16[1,130,128]{2,1,0:T(8,128)(2,1)S(1)} %get-tuple-element.34, ...), kind=kLoop, calls=%fused_computation.48 | loop fusion | flops 34344960 | bytes 12912640 | tf_op jit(solution)/shard_map/concatenate | solution.py:74
  39.2 23.4 %multiply_reduce_fusion.1 = (f32[128,128]{1,0:T(8,128)S(1)}, f32[128,128,128]{2,1,0:T(8,128)S(1)}) fusion(bf16[129,130,128]{2,1,0:T(8,128)(2,1)S(1)} %get-tuple-element.16, f32[128]{0:T(128)S(1)} %get-tuple-element.43, f32[128,128]{1,0:T(8,128)S(1)} %get-tuple-element.30, f32[128]{0:T(128)S(1)} %get-tuple-element.44, f32[128,128]{1,0:T(8,128)S(1)} %get-tuple-element.31, ...), kind=kLoop, calls=%fused_computation.46 | loop fusion | flops 90161152 | bytes 38474240 | tf_op jit(solution)/shard_map/reduce_sum | solution.py:46
  62.7 4.3 %multiply_convert_fusion.1 = bf16[128,128,128]{2,1,0:T(8,128)(2,1)} fusion(f32[128,128,128]{2,1,0:T(8,128)S(1)} %get-tuple-element.10, f32[128]{0:T(128)S(1)} %get-tuple-element.63, f32[128,128]{1,0:T(8,128)S(1)} %add_rsqrt_fusion.1), kind=kLoop, calls=%fused_computation.45 | loop fusion | flops 6291456 | bytes 12648960 | tf_op jit(solution)/shard_map/convert_element_type | solution.py:47
  67.0 2.4 %slice_reduce_fusion = (bf16[128,7,128]{2,1,0:T(8,128)(2,1)S(1)}, bf16[128,7,128]{2,1,0:T(8,128)(2,1)S(1)}) fusion(bf16[2,128,7,128]{3,0,2,1:T(2,128)(2,1)S(1)} %bitcast.145), kind=kLoop, calls=%fused_computation.56 | loop fusion | bytes 917504 | tf_op jit(solution)/shard_map/slice | solution.py:96
  69.4 0.1 reshape_squeeze.6
  69.5 3.4 %fusion.26 = bf16[16384,128]{1,0:T(8,128)(2,1)S(1)} fusion(bf16[16384,128]{1,0:T(8,128)(2,1)} %bitcast.143, f32[128]{0:T(128)S(1)} %get-tuple-element.59, bf16[7,128,128]{2,1,0:T(8,128)(2,1)S(1)} %reshape_squeeze.6), kind=kOutput, calls=%fused_computation.36 | convolution fusion | flops 541065216 | bytes 8421888 | tf_op jit(solution)/shard_map/dot_general | solution.py:49
  73.0 1.2 fusion.34
  74.2 1.2 fusion.35
  75.4 0.0 copy-start.3
  75.4 4.5 %convolution_add_fusion.5 = f32[16384,128]{1,0:T(8,128)} fusion(bf16[16384,128]{1,0:T(8,128)(2,1)S(1)} %fusion.26, f32[128]{0:T(128)S(1)} %get-tuple-element.57, bf16[7,128,128]{2,1,0:T(8,128)(2,1)S(1)} %reshape_squeeze.6), kind=kOutput, calls=%fused_computation.25 | convolution fusion | flops 538968064 | bytes 12616192 | tf_op jit(solution)/shard_map/dot_general | solution.py:63
  79.9 4.5 %fusion.29 = f32[16384,128]{1,0:T(8,128)} fusion(f32[16384,128]{1,0:T(8,128)S(1)} %fusion.34, bf16[16384,128]{1,0:T(8,128)(2,1)S(1)} %bitcast.140, f32[128]{0:T(128)S(1)} %get-tuple-element.56, bf16[7,128,128]{2,1,0:T(8,128)(2,1)S(1)} %reshape_squeeze.6), kind=kOutput, calls=%fused_computation.39 | convolution fusion | flops 547356672 | bytes 21004800 | tf_op jit(solution)/shard_map/dot_general | solution.py:59
  84.4 4.6 %fusion.28 = f32[16384,128]{1,0:T(8,128)} fusion(f32[16384,128]{1,0:T(8,128)S(1)} %fusion.35, bf16[16384,128]{1,0:T(8,128)(2,1)S(1)} %bitcast.141, f32[128]{0:T(128)S(1)} %get-tuple-element.58, bf16[7,128,128]{2,1,0:T(8,128)(2,1)S(1)} %reshape_squeeze.6), kind=kOutput, calls=%fused_computation.38 | convolution fusion | flops 547356672 | bytes 21004800 | tf_op jit(solution)/shard_map/dot_general | solution.py:54
  89.0 9.8 %fusion.25 = bf16[16384,128]{1,0:T(8,128)(2,1)S(1)} fusion(f32[16384,128]{1,0:T(8,128)} %convolution_add_fusion.5, f32[16384,128]{1,0:T(8,128)} %fusion.29, bf16[16384,128]{1,0:T(8,128)(2,1)S(1)} %bitcast.142, f32[16384,128]{1,0:T(8,128)} %fusion.28, bf16[7,128,128]{2,1,0:T(8,128)(2,1)S(1)} %reshape_squeeze.6), kind=kOutput, calls=%fused_computation.35 | convolution fusion | flops 553648128 | bytes 37781504 | tf_op jit(solution)/shard_map/dot_general | solution.py:65
  98.8 0.0 copy-start
  98.8 0.1 fusion.36
  98.9 4.6 %collective-permute-start.5 = (bf16[128,1,128]{2,1,0:T(2,128)(2,1)S(1)}, bf16[128,1,128]{2,1,0:T(2,128)(2,1)S(1)}, u32[]{:S(2)}, u32[]{:S(2)}) collective-permute-start(bf16[128,1,128]{2,1,0:T(2,128)(2,1)S(1)} %get-tuple-element.19), channel_id=1, source_target_pairs={{0,1},{1,2},{2,3},{3,4},{4,5},{5,6},{6,7},{7,8},{8,9},{9,10},{10,1... | collective-permute-start | bytes 98312 | tf_op jit(solution)/shard_map/ppermute | solution.py:19
  103.5 1.3 collective-permute-done.5
  104.9 6.0 %collective-permute-done.6 = bf16[128,1,128]{2,1,0:T(2,128)(2,1)S(1)} collective-permute-done((bf16[128,1,128]{2,1,0:T(2,128)(2,1)S(1)}, bf16[128,1,128]{2,1,0:T(2,128)(2,1)S(1)}, u32[]{:S(2)}, u32[]{:S(2)}) %collective-permute-start.6) | collective-permute-done | bytes 32800 | tf_op jit(solution)/shard_map/ppermute | solution.py:21
  110.9 0.1 collective-permute-start.7
  111.0 4.5 %collective-permute-start.8 = (bf16[1,130,128]{2,1,0:T(8,128)(2,1)S(1)}, bf16[1,130,128]{2,1,0:T(8,128)(2,1)S(1)}, u32[]{:S(2)}, u32[]{:S(2)}) collective-permute-start(bf16[1,130,128]{2,1,0:T(8,128)(2,1)S(1)} %get-tuple-element.13), channel_id=1, source_target_pairs={{0,16},{16,32},{32,48},{48,64},{64,80},{80,96},{96,112},{1,17},{17... | collective-permute-start | bytes 99848 | tf_op jit(solution)/shard_map/ppermute | solution.py:19
  115.5 1.3 collective-permute-start.9
  116.8 0.1 reshape_squeeze.7
  116.9 0.0 copy-start.1
  116.9 4.0 %collective-permute-done.9 = bf16[1,130,128]{2,1,0:T(8,128)(2,1)S(1)} collective-permute-done((bf16[1,130,128]{2,1,0:T(8,128)(2,1)S(1)}, bf16[1,130,128]{2,1,0:T(8,128)(2,1)S(1)}, u32[]{:S(2)}, u32[]{:S(2)}) %collective-permute-start.9) | collective-permute-done | bytes 33312 | tf_op jit(solution)/shard_map/ppermute | solution.py:21
  120.9 9.7 %maximum_maximum_fusion.1 = (bf16[129,130,128]{2,1,0:T(8,128)(2,1)S(1)}, bf16[129,130,128]{2,1,0:T(8,128)(2,1)S(1)}) fusion(bf16[128,1,128]{2,1,0:T(2,128)(2,1)S(1)} %collective-permute-done.6, bf16[128,128,128]{2,1,0:T(8,128)(2,1)} %bitcast.138, bf16[128,1,128]{2,1,0:T(2,128)(2,1)S(1)} %collective-permute-done.5, ...), kind=kLoop, calls=%fused_computation.50 | loop fusion | flops 34344960 | bytes 12912640 | tf_op jit(solution)/shard_map/concatenate | solution.py:74
  130.6 23.3 %multiply_reduce_fusion = (f32[128,128]{1,0:T(8,128)S(1)}, f32[128,128,128]{2,1,0:T(8,128)S(1)}) fusion(bf16[129,130,128]{2,1,0:T(8,128)(2,1)S(1)} %get-tuple-element.12, f32[128]{0:T(128)S(1)} %get-tuple-element.52, f32[128,128]{1,0:T(8,128)S(1)} %get-tuple-element.30, f32[128]{0:T(128)S(1)} %get-tuple-element.53, f32[128,128]{1,0:T(8,128)S(1)} %get-tuple-element.31, ...), kind=kLoop, calls=%fused_computation.43 | loop fusion | flops 90161152 | bytes 38474240 | tf_op jit(solution)/shard_map/reduce_sum | solution.py:46
  154.0 4.7 %multiply_convert_fusion = bf16[128,128,128]{2,1,0:T(8,128)(2,1)S(1)} fusion(f32[128,128,128]{2,1,0:T(8,128)S(1)} %get-tuple-element.8, f32[128]{0:T(128)S(1)} %get-tuple-element.62, f32[128,128]{1,0:T(8,128)S(1)} %add_rsqrt_fusion), kind=kLoop, calls=%fused_computation.42 | loop fusion | flops 6291456 | bytes 12648960 | tf_op jit(solution)/shard_map/convert_element_type | solution.py:47
  158.7 1.2 fusion.27
  160.0 1.2 fusion.32
  161.2 1.2 fusion.33
  162.4 4.5 %convolution_add_fusion.1 = f32[16384,128]{1,0:T(8,128)} fusion(bf16[16384,128]{1,0:T(8,128)(2,1)S(1)} %fusion.27, f32[128]{0:T(128)S(1)} %get-tuple-element.61, bf16[7,128,128]{2,1,0:T(8,128)(2,1)S(1)} %reshape_squeeze.7), kind=kOutput, calls=%fused_computation.9 | convolution fusion | flops 538968064 | bytes 12616192 | tf_op jit(solution)/shard_map/dot_general | solution.py:63
  166.9 4.5 %fusion.31 = f32[16384,128]{1,0:T(8,128)} fusion(f32[16384,128]{1,0:T(8,128)S(1)} %fusion.32, bf16[16384,128]{1,0:T(8,128)(2,1)S(1)} %copy-done.1, f32[128]{0:T(128)S(1)} %get-tuple-element.60, bf16[7,128,128]{2,1,0:T(8,128)(2,1)S(1)} %reshape_squeeze.7), kind=kOutput, calls=%fused_computation.41 | convolution fusion | flops 547356672 | bytes 21004800 | tf_op jit(solution)/shard_map/dot_general | solution.py:59
  171.4 4.5 %fusion.30 = f32[16384,128]{1,0:T(8,128)} fusion(f32[16384,128]{1,0:T(8,128)S(1)} %fusion.33, bf16[16384,128]{1,0:T(8,128)(2,1)S(1)} %copy-done.1, f32[128]{0:T(128)S(1)} %get-tuple-element.54, bf16[7,128,128]{2,1,0:T(8,128)(2,1)S(1)} %reshape_squeeze.7), kind=kOutput, calls=%fused_computation.40 | convolution fusion | flops 547356672 | bytes 21004800 | tf_op jit(solution)/shard_map/dot_general | solution.py:54
  176.0 11.8 %fusion.24 = bf16[16384,128]{1,0:T(8,128)(2,1)} fusion(f32[16384,128]{1,0:T(8,128)} %convolution_add_fusion.1, f32[16384,128]{1,0:T(8,128)} %fusion.31, bf16[16384,128]{1,0:T(8,128)(2,1)S(1)} %copy-done.1, f32[16384,128]{1,0:T(8,128)} %fusion.30, bf16[7,128,128]{2,1,0:T(8,128)(2,1)S(1)} %reshape_squeeze.7), kind=kOutput, calls=%fused_computation.34 | convolution fusion | flops 553648128 | bytes 37781504 | tf_op jit(solution)/shard_map/dot_general | solution.py:65
  (20 shorter events, 0.2 us)
Async XLA Ops:
  1.1 18.3 %collective-permute-start = (bf16[128,1,128]{2,1,0:T(2,128)(2,1)S(1)}, bf16[128,1,128]{2,1,0:T(2,128)(2,1)S(1)}, u32[]{:S(2)}, u32[]{:S(2)}) collective-permute-start(bf16[128,1,128]{2,1,0:T(2,128)(2,1)S(1)} %get-tuple-element.21), channel_id=1, source_target_pairs={{0,1},{1,2},{2,3},{3,4},{4,5},{5,6},{6,7},{7,8},{8,9},{9,10},{10,1... | collective-permute-start | bytes 98312 | tf_op jit(solution)/shard_map/ppermute | solution.py:19
  5.3 14.2 %collective-permute-start.1 = (bf16[128,1,128]{2,1,0:T(2,128)(2,1)S(1)}, bf16[128,1,128]{2,1,0:T(2,128)(2,1)S(1)}, u32[]{:S(2)}, u32[]{:S(2)}) collective-permute-start(bf16[128,1,128]{2,1,0:T(2,128)(2,1)S(1)} %get-tuple-element.22), channel_id=1, source_target_pairs={{1,0},{2,1},{3,2},{4,3},{5,4},{6,5},{7,6},{8,7},{9,8},{10,9},{11,1... | collective-permute-start | bytes 98312 | tf_op jit(solution)/shard_map/ppermute | solution.py:21
  7.0 60.0 %all-to-all-start = ((bf16[128,2,7,128]{3,1,2,0:T(2,128)(2,1)}), bf16[128,2,7,128]{3,1,2,0:T(2,128)(2,1)S(1)}, u32[]{:S(2)}, u32[]{:S(2)}) async-start(bf16[128,2,7,128]{3,1,2,0:T(2,128)(2,1)} %stack.7), calls=%async_computation | async-start | bytes 917504 | tf_op jit(solution)/shard_map/all_to_all | solution.py:87
  20.3 8.4 %collective-permute-start.3 = (bf16[1,130,128]{2,1,0:T(8,128)(2,1)S(1)}, bf16[1,130,128]{2,1,0:T(8,128)(2,1)S(1)}, u32[]{:S(2)}, u32[]{:S(2)}) collective-permute-start(bf16[1,130,128]{2,1,0:T(8,128)(2,1)S(1)} %get-tuple-element.17), channel_id=1, source_target_pairs={{0,16},{16,32},{32,48},{48,64},{64,80},{80,96},{96,112},{1,17},{17... | collective-permute-start | bytes 99848 | tf_op jit(solution)/shard_map/ppermute | solution.py:19
  23.6 5.1 %collective-permute-start.4 = (bf16[1,130,128]{2,1,0:T(8,128)(2,1)S(1)}, bf16[1,130,128]{2,1,0:T(8,128)(2,1)S(1)}, u32[]{:S(2)}, u32[]{:S(2)}) collective-permute-start(bf16[1,130,128]{2,1,0:T(8,128)(2,1)S(1)} %get-tuple-element.18), channel_id=1, source_target_pairs={{16,0},{32,16},{48,32},{64,48},{80,64},{96,80},{112,96},{17,1},{33... | collective-permute-start | bytes 99848 | tf_op jit(solution)/shard_map/ppermute | solution.py:21
  24.9 4.7 %collective-permute-start.2 = (bf16[2,130,128]{2,1,0:T(8,128)(2,1)S(1)}, bf16[2,130,128]{2,1,0:T(8,128)(2,1)S(1)}, u32[]{:S(2)}, u32[]{:S(2)}) collective-permute-start(bf16[2,130,128]{2,1,0:T(8,128)(2,1)S(1)} %pad_maximum_fusion.6), channel_id=1, source_target_pairs={{8,0},{9,1},{10,2},{11,3},{12,4},{13,5},{14,6},{15,7},{0,8},{1,9},... | collective-permute-start | bytes 199688 | tf_op jit(solution)/shard_map/ppermute | solution.py:31
  28.6 10.6 %copy-start.2 = (bf16[128,128,128]{2,1,0:T(8,128)(2,1)S(1)}, bf16[128,128,128]{2,1,0:T(8,128)(2,1)}, u32[]{:S(2)}) copy-start(bf16[128,128,128]{2,1,0:T(8,128)(2,1)} %param.6) | copy-start | bytes 12582916
  75.4 4.5 %copy-start.3 = (bf16[128,128,128]{2,1,0:T(8,128)(2,1)S(1)}, bf16[128,128,128]{2,1,0:T(8,128)(2,1)}, u32[]{:S(2)}) copy-start(bf16[128,128,128]{2,1,0:T(8,128)(2,1)} %param.6) | copy-start | bytes 12582916
  98.8 12.1 %copy-start = (bf16[16384,128]{1,0:T(8,128)(2,1)}, bf16[16384,128]{1,0:T(8,128)(2,1)S(1)}, u32[]{:S(2)}) copy-start(bf16[16384,128]{1,0:T(8,128)(2,1)S(1)} %fusion.25) | copy-start | bytes 12582916
  98.9 6.0 %collective-permute-start.5 = (bf16[128,1,128]{2,1,0:T(2,128)(2,1)S(1)}, bf16[128,1,128]{2,1,0:T(2,128)(2,1)S(1)}, u32[]{:S(2)}, u32[]{:S(2)}) collective-permute-start(bf16[128,1,128]{2,1,0:T(2,128)(2,1)S(1)} %get-tuple-element.19), channel_id=1, source_target_pairs={{0,1},{1,2},{2,3},{3,4},{4,5},{5,6},{6,7},{7,8},{8,9},{9,10},{10,1... | collective-permute-start | bytes 98312 | tf_op jit(solution)/shard_map/ppermute | solution.py:19
  103.5 7.3 %collective-permute-start.6 = (bf16[128,1,128]{2,1,0:T(2,128)(2,1)S(1)}, bf16[128,1,128]{2,1,0:T(2,128)(2,1)S(1)}, u32[]{:S(2)}, u32[]{:S(2)}) collective-permute-start(bf16[128,1,128]{2,1,0:T(2,128)(2,1)S(1)} %get-tuple-element.20), channel_id=1, source_target_pairs={{1,0},{2,1},{3,2},{4,3},{5,4},{6,5},{7,6},{8,7},{9,8},{10,9},{11,1... | collective-permute-start | bytes 98312 | tf_op jit(solution)/shard_map/ppermute | solution.py:21
  110.9 10.0 %collective-permute-start.7 = (bf16[2,130,128]{2,1,0:T(8,128)(2,1)S(1)}, bf16[2,130,128]{2,1,0:T(8,128)(2,1)S(1)}, u32[]{:S(2)}, u32[]{:S(2)}) collective-permute-start(bf16[2,130,128]{2,1,0:T(8,128)(2,1)S(1)} %pad_maximum_fusion.7), channel_id=1, source_target_pairs={{8,0},{9,1},{10,2},{11,3},{12,4},{13,5},{14,6},{15,7},{0,8},{1,9},... | collective-permute-start | bytes 199688 | tf_op jit(solution)/shard_map/ppermute | solution.py:31
  111.0 5.9 %collective-permute-start.8 = (bf16[1,130,128]{2,1,0:T(8,128)(2,1)S(1)}, bf16[1,130,128]{2,1,0:T(8,128)(2,1)S(1)}, u32[]{:S(2)}, u32[]{:S(2)}) collective-permute-start(bf16[1,130,128]{2,1,0:T(8,128)(2,1)S(1)} %get-tuple-element.13), channel_id=1, source_target_pairs={{0,16},{16,32},{32,48},{48,64},{64,80},{80,96},{96,112},{1,17},{17... | collective-permute-start | bytes 99848 | tf_op jit(solution)/shard_map/ppermute | solution.py:19
  115.5 5.4 %collective-permute-start.9 = (bf16[1,130,128]{2,1,0:T(8,128)(2,1)S(1)}, bf16[1,130,128]{2,1,0:T(8,128)(2,1)S(1)}, u32[]{:S(2)}, u32[]{:S(2)}) collective-permute-start(bf16[1,130,128]{2,1,0:T(8,128)(2,1)S(1)} %get-tuple-element.14), channel_id=1, source_target_pairs={{16,0},{32,16},{48,32},{64,48},{80,64},{96,80},{112,96},{17,1},{33... | collective-permute-start | bytes 99848 | tf_op jit(solution)/shard_map/ppermute | solution.py:21
  116.9 13.7 %copy-start.1 = (bf16[16384,128]{1,0:T(8,128)(2,1)S(1)}, bf16[16384,128]{1,0:T(8,128)(2,1)}, u32[]{:S(2)}) copy-start(bf16[16384,128]{1,0:T(8,128)(2,1)} %copy-done) | copy-start | bytes 12582916
